TPU v7x, 256 devices: a whole 4x4x8 slice. The times are simulated.
256 devices in a mesh: section: 8 (over z), expert: 2 (over core), tensor: 16 (over y, x).
Axes of the slice: x: 4, y: 4, z: 8, core: 2. Of those that a mesh axis runs over, the one named last changes fastest.
Arguments:
- tokens: bfloat16 [8192, 6144], P(('section', 'expert'), 'tensor'), may hold values from -6 to 6
- norm_gain: float32 [4, 6144], P(None, 'tensor'), may hold values from 0.5 to 1.5
- router: float32 [4, 6144, 8], P(None, 'tensor'), may hold values from -0.078125 to 0.078125
- w_gate: bfloat16 [8, 2, 6144, 4096], P('section', 'expert', None, 'tensor'), may hold values from -0.078125 to 0.078125
- w_up: bfloat16 [8, 2, 6144, 4096], P('section', 'expert', None, 'tensor'), may hold values from -0.078125 to 0.078125
- w_down: bfloat16 [8, 2, 4096, 6144], P('section', 'expert', 'tensor'), may hold values from -0.0625 to 0.0625
- expert_ids: int32 [2, 8192, 2], P(None, ('section', 'expert')), may hold values from 0 to 7, all different within a row
- lengths: int32 [8, 8], P(None, 'expert'), may hold values from 32 to 128
Outputs:
- encoded: bfloat16 [8192, 6144], P(('section', 'expert'), 'tensor')
All inputs are finite; a program needn't handle non-finite values.
Results may differ from a plain program's by a relative error of at most 0.006.
Values may be sent and summed in bfloat16 or wider, within the bound.
A program may use at most 64 MiB of HBM per device.

v0:
```python
import jax
import jax.numpy as jnp
from jax import lax
from jax.sharding import PartitionSpec as P

D = 6144
E = 8
EXP_WIN = 2
SEQ_LEN = 128
STEPS = 2
CAP = 64
norm_eps = 1e-05


def swapped(x, axis, bit):
    return lax.ppermute(x, axis, [(i, i ^ 1 << bit) for i in range(lax.axis_size(axis))])


def from_behind(x, axis, by):
    peers = lax.axis_size(axis)
    return lax.ppermute(x, axis, [(i, (i + by) % peers) for i in range(peers)])


def route_tables(choice_ids, seq_lens, gate_logits):
    token_count = choice_ids.shape[0]
    expert_range = jnp.arange(E, dtype=jnp.int32)
    match_ids = choice_ids[:, :, None] == expert_range[None, None, :]
    one_hot = match_ids.astype(jnp.float32)
    picked = jnp.sum(gate_logits[:, None, :] * one_hot, axis=2)
    first_weight = jax.nn.sigmoid(picked[:, 0] - picked[:, 1])
    second_weight = jax.nn.sigmoid(picked[:, 1] - picked[:, 0])
    dense_gates = (
        first_weight[:, None] * one_hot[:, 0, :] + second_weight[:, None] * one_hot[:, 1, :]
    )
    dense_gates = dense_gates[:, :EXP_WIN]
    positions = jnp.arange(token_count, dtype=jnp.int32)
    live_rows = positions % SEQ_LEN < jnp.repeat(seq_lens, SEQ_LEN, total_repeat_length=token_count)
    named = jnp.any(match_ids, axis=1)[:, :EXP_WIN] & live_rows[:, None]
    named_int = named.astype(jnp.int32)
    earlier = jnp.cumsum(named_int, axis=0) - named_int
    slot_range = jnp.arange(CAP, dtype=jnp.int32)
    placed = named[None, :, :] & (earlier[None, :, :] == slot_range[:, None, None])
    route_table = jnp.transpose(placed.astype(jnp.float32), (2, 0, 1))
    return (route_table, route_table * jnp.transpose(dense_gates)[:, None, :])


def moe_layer(
    layer_rows, gain_row, router_matrix, gate_w, up_w, down_w, choice_ids, seq_lens, expert_count
):
    as_float = layer_rows.astype(jnp.float32)
    scaled = as_float * gain_row[None, :]
    part_logits = jnp.dot(scaled, router_matrix, precision=lax.Precision.HIGHEST)
    square_sum, logit_sum = lax.psum((jnp.sum(as_float * as_float, axis=1), part_logits), "tensor")
    inv_rms = lax.rsqrt(square_sum / D + norm_eps)
    normed = (scaled * inv_rms[:, None]).astype(jnp.bfloat16)
    gate_logits = inv_rms[:, None] * logit_sum
    route_table, weighted = route_tables(choice_ids, seq_lens, gate_logits)
    fsplit_count = expert_count // EXP_WIN
    table_narrow = route_table.astype(jnp.bfloat16)
    feature_count = normed.shape[1]
    picked_rows = jnp.einsum(
        "ecr,rd->ecd", table_narrow, normed, preferred_element_type=jnp.float32
    ).astype(jnp.bfloat16)
    widened = jnp.broadcast_to(picked_rows[:, None], (EXP_WIN, fsplit_count, CAP, feature_count))
    arrived = lax.all_to_all(
        widened.reshape(expert_count, CAP, feature_count),
        "expert",
        split_axis=0,
        concat_axis=1,
        tiled=True,
    )
    partner = swapped(arrived, "section", 0)
    held_rows = jnp.concatenate([arrived, partner], axis=1)
    feature_piece = lax.all_gather(held_rows, "tensor", axis=2, tiled=True)
    col_count = feature_piece.shape[2]
    gate_part = lax.slice_in_dim(gate_w, 0, col_count, axis=1)
    up_part = lax.slice_in_dim(up_w, 0, col_count, axis=1)
    gate_more = jnp.einsum(
        "snd,sdf->snf", feature_piece, gate_part, preferred_element_type=jnp.float32
    )
    up_more = jnp.einsum("snd,sdf->snf", feature_piece, up_part, preferred_element_type=jnp.float32)
    hidden = (jax.nn.silu(gate_more) * up_more).astype(jnp.bfloat16)
    partial_out = jnp.einsum("snf,sfd->snd", hidden, down_w, preferred_element_type=jnp.float32)
    summed = lax.psum_scatter(
        partial_out.astype(jnp.bfloat16), "tensor", scatter_dimension=2, tiled=True
    )
    own_count = summed.shape[1] // 2
    own_part = summed[:, :own_count]
    other_part = summed[:, own_count:]
    from_partner = swapped(other_part, "section", 0)
    slab_out = (own_part.astype(jnp.float32) + from_partner.astype(jnp.float32)).astype(
        jnp.bfloat16
    )
    returned = lax.all_to_all(slab_out, "expert", split_axis=1, concat_axis=0, tiled=True)
    half_width = returned.shape[2]
    per_expert = jnp.sum(
        returned.reshape(EXP_WIN, fsplit_count, CAP, half_width).astype(jnp.float32), axis=1
    )
    mixture = jnp.einsum("ecr,ecd->rd", weighted, per_expert, precision=lax.Precision.HIGHEST)
    return (as_float + mixture).astype(jnp.bfloat16)


def on_device(tokens, norm_gain, router, w_gate, w_up, w_down, expert_ids, lengths):
    section_count = lax.axis_size("section")
    section_place = lax.axis_index("section")
    expert_count = lax.axis_size("expert")
    layer_place = section_place // 2
    gain_row = lax.dynamic_index_in_dim(norm_gain, layer_place, 0, keepdims=False)
    router_matrix = lax.dynamic_index_in_dim(router, layer_place, 0, keepdims=False)
    current = tokens
    for step_index in range(STEPS):
        micro_batch = (section_place - 2 * step_index) % section_count
        seq_lens = lax.dynamic_index_in_dim(lengths, micro_batch, 0, keepdims=False)
        current = moe_layer(
            current,
            gain_row,
            router_matrix,
            w_gate[0],
            w_up[0],
            w_down[0],
            expert_ids[step_index],
            seq_lens,
            expert_count,
        )
        if step_index + 1 < STEPS:
            current = from_behind(current, "section", 2)
    return current


def solution(mesh):
    in_specs = (
        P(("section", "expert"), "tensor"),
        P(None, "tensor"),
        P(None, "tensor", None),
        P("section", "expert", None, "tensor"),
        P("section", "expert", None, "tensor"),
        P("section", "expert", "tensor", None),
        P(None, ("section", "expert"), None),
        P(None, "expert"),
    )
    out_specs = P(("section", "expert"), "tensor")
    return jax.shard_map(
        on_device, mesh=mesh, in_specs=in_specs, out_specs=out_specs, check_vma=False
    )
```

profile of v0, /device:TPU:1, one launch (start us, length us, event | category | flops | bytes accessed | tf_op | source)
XLA Modules:
  0.0 600.9 jit_solution(5741067348918299058)
XLA Ops:
  6.5 1.3 fusion.26
  9.3 1.8 fusion.21
  11.1 61.2 %all-reduce.1 = (f32[512]{0:T(512)S(1)}, f32[512,8]{0,1:T(8,128)}) all-reduce(f32[512]{0:T(512)S(1)} %fusion.26, f32[512,8]{0,1:T(8,128)S(1)} %fusion.21), channel_id=1, replica_groups=mesh['section'=8,'expert'=2,'tensor'=16] {'tensor'}, use_global_device_ids=true, to_apply=%region_4.6 | all-reduce | flops 4608 | bytes 36864 | tf_op jit(solution)/shard_map/psum | solution.py:53
  72.3 1.0 dynamic-slice_reduce_fusion
  74.6 2.5 select_compare_fusion.1
  78.9 1.3 convolution_convert_fusion.3
  80.2 18.3 %all_to_all.42 = bf16[2,64,384]{2,1,0:T(8,128)(2,1)S(1)} all-to-all(bf16[2,64,384]{2,1,0:T(8,128)(2,1)S(1)} %convolution_convert_fusion.3), channel_id=1, replica_groups=mesh['section'=8,'expert'=2,'tensor'=16] {'expert'}, dimensions={0} | all-to-all | bytes 196608 | tf_op jit(solution)/shard_map/all_to_all | solution.py:65
  98.5 1.6 collective-permute-start
  100.2 2.7 collective-permute-done
  103.7 53.6 %all-gather.3.cloned.1.call-done = bf16[1,256,6144]{2,1,0:T(8,128)(2,1)} async-done(((bf16[1,256,384]{2,1,0:T(8,128)(2,1)}), bf16[1,256,6144]{2,1,0:T(8,128)(2,1)}) %all-gather.3.cloned.1.call-update) | async-done | bytes 3145744 | tf_op jit(solution)/shard_map/all_gather | solution.py:74
  157.3 3.8 fusion.9
  161.1 8.0 %fusion = bf16[1,256,6144]{2,1,0:T(8,128)(2,1)} fusion(bf16[1,1,256,6144]{3,2,1,0:T(8,128)(2,1)S(1)} %copy-done, f32[256,256]{1,0:T(8,128)S(1)} %fusion.9, bf16[1,1,6144,256]{3,2,1,0:T(8,128)(2,1)} %param.17, bf16[1,256,6144]{2,1,0:T(8,128)(2,1)} %all-gather.3.cloned.1.call-done), kind=kOutput, calls=%fused_computation.2 | convolution fusion | flops 1612578816 | bytes 12845056 | tf_op jit(solution)/shard_map/snf,sfd->snd/dot_general | solution.py:83
  169.1 13.9 %copy.13 = bf16[1,256,6144]{1,0,2:T(2,128)(2,1)} copy(bf16[1,256,6144]{2,1,0:T(8,128)(2,1)} %fusion) | data formatting | bytes 6291456
  183.1 5.0 copy.34
  188.2 2.6 select_compare_fusion
  192.0 0.7 broadcast_multiply_fusion.1
  192.8 0.7 slice_bitcast_fusion.3
  194.1 75.0 %reduce-scatter.7.cloned.1.call-done = bf16[384,256]{1,0:T(8,128)(2,1)} async-done(((bf16[6144,256]{1,0:T(8,128)(2,1)}), bf16[384,256]{1,0:T(8,128)(2,1)}) %reduce-scatter.7.cloned.1.call-update) | async-done | bytes 196624
  269.1 1.1 reshape_bitcast_fusion.1
  270.2 1.1 fusion.103
  271.4 1.7 copy.22
  273.1 1.3 collective-permute-start.1
  274.6 0.8 reduce-window.27
  275.3 1.7 copy.21
  277.0 1.0 add_convert_fusion.1
  278.0 0.8 copy.36
  279.4 2.7 reduce.13
  282.1 1.6 reshape.217
  283.6 8.5 %all_to_all.43 = bf16[2,2,12288]{2,1,0:T(2,128)(2,1)} all-to-all(bf16[2,2,12288]{2,1,0:T(2,128)(2,1)} %reshape.217), channel_id=1, replica_groups=mesh['section'=8,'expert'=2,'tensor'=16] {'expert'}, dimensions={0} | all-to-all | bytes 196608 | tf_op jit(solution)/shard_map/all_to_all | solution.py:94
  292.2 1.7 reshape.218
  293.8 0.9 copy.18
  294.8 1.2 fusion.19
  296.0 2.3 collective-permute-start.2
  298.4 0.7 add_bitcast_fusion
  299.7 14.5 %collective-permute-done.2 = bf16[512,384]{1,0:T(8,128)(2,1)S(1)} collective-permute-done((bf16[512,384]{1,0:T(8,128)(2,1)S(1)}, bf16[512,384]{1,0:T(8,128)(2,1)S(1)}, u32[]{:S(2)}, u32[]{:S(2)}) %collective-permute-start.2) | collective-permute-done | bytes 393248 | tf_op jit(solution)/shard_map/ppermute | solution.py:21
  314.2 0.7 fusion.27
  314.9 1.5 fusion.23
  316.4 58.0 %all-reduce = (f32[512]{0:T(512)}, f32[512,8]{0,1:T(8,128)}) all-reduce(f32[512]{0:T(512)} %fusion.27, f32[512,8]{0,1:T(8,128)S(1)} %fusion.23), channel_id=1, replica_groups=mesh['section'=8,'expert'=2,'tensor'=16] {'tensor'}, use_global_device_ids=true, to_apply=%region_12.14 | all-reduce | flops 4608 | bytes 36864 | tf_op jit(solution)/shard_map/psum | solution.py:53
  375.1 1.0 convolution_convert_fusion.2
  376.1 18.4 %all_to_all.44 = bf16[2,64,384]{2,1,0:T(8,128)(2,1)S(1)} all-to-all(bf16[2,64,384]{2,1,0:T(8,128)(2,1)S(1)} %convolution_convert_fusion.2), channel_id=1, replica_groups=mesh['section'=8,'expert'=2,'tensor'=16] {'expert'}, dimensions={0} | all-to-all | bytes 196608 | tf_op jit(solution)/shard_map/all_to_all | solution.py:65
  394.6 4.4 collective-permute-start.3
  398.9 2.8 collective-permute-done.3
  402.5 52.4 %all-gather.5.cloned.1.call-done = bf16[1,256,6144]{2,1,0:T(8,128)(2,1)} async-done(((bf16[1,256,384]{2,1,0:T(8,128)(2,1)}), bf16[1,256,6144]{2,1,0:T(8,128)(2,1)}) %all-gather.5.cloned.1.call-update) | async-done | bytes 3145744 | tf_op jit(solution)/shard_map/all_gather | solution.py:74
  454.9 4.5 fusion.2
  459.4 8.0 %fusion.1 = bf16[1,256,6144]{2,1,0:T(8,128)(2,1)} fusion(bf16[1,1,256,6144]{3,2,1,0:T(8,128)(2,1)S(1)} %copy-done, f32[256,256]{1,0:T(8,128)} %fusion.2, bf16[1,256,6144]{2,1,0:T(8,128)(2,1)} %all-gather.5.cloned.1.call-done, bf16[1,1,6144,256]{3,2,1,0:T(8,128)(2,1)} %param.17), kind=kOutput, calls=%fused_computation.3 | convolution fusion | flops 1612578816 | bytes 12845056 | tf_op jit(solution)/shard_map/snf,sfd->snd/dot_general | solution.py:83
  467.4 13.9 %copy.15 = bf16[1,256,6144]{1,0,2:T(2,128)(2,1)} copy(bf16[1,256,6144]{2,1,0:T(8,128)(2,1)} %fusion.1) | data formatting | bytes 6291456
  481.4 5.0 copy.33
  486.4 1.3 slice_bitcast_fusion.1
  487.7 0.7 broadcast_multiply_fusion
  488.5 78.9 %reduce-scatter.9.cloned.1.call-done = bf16[384,256]{1,0:T(8,128)(2,1)} async-done(((bf16[6144,256]{1,0:T(8,128)(2,1)}), bf16[384,256]{1,0:T(8,128)(2,1)}) %reduce-scatter.9.cloned.1.call-update) | async-done | bytes 196624
  567.4 1.1 reshape_bitcast_fusion
  568.5 1.1 fusion.102
  569.7 1.7 copy.24
  571.3 1.3 collective-permute-start.4
  572.6 0.7 fusion.85
  573.3 1.7 copy.23
  575.1 1.0 add_convert_fusion
  576.1 0.8 copy.35
  576.9 2.7 reduce.14
  579.6 1.6 reshape.219
  581.2 8.7 %all_to_all.45 = bf16[2,2,12288]{2,1,0:T(2,128)(2,1)} all-to-all(bf16[2,2,12288]{2,1,0:T(2,128)(2,1)} %reshape.219), channel_id=1, replica_groups=mesh['section'=8,'expert'=2,'tensor'=16] {'expert'}, dimensions={0} | all-to-all | bytes 196608 | tf_op jit(solution)/shard_map/all_to_all | solution.py:94
  589.8 1.7 reshape.220
  591.5 0.9 copy.20
  592.4 2.0 fusion.18
  (58 shorter events, 10.1 us)
Async XLA Ops:
  6.5 154.6 %copy-start = (bf16[1,1,256,6144]{3,2,1,0:T(8,128)(2,1)S(1)}, bf16[1,1,256,6144]{3,2,1,0:T(8,128)(2,1)}, u32[]{:S(2)}) copy-start(bf16[1,1,256,6144]{3,2,1,0:T(8,128)(2,1)} %param.19) | copy-start | bytes 9437188
  6.5 150.7 %all-gather.3.cloned.1.call-start = ((), (), s32[]{:S(2)}) async-start(), calls=%async_computation.6 | async-start | bytes 3342336 | tf_op jit(solution)/shard_map/all_gather | solution.py:74
  8.5 95.1 %copy-start.2 = (s32[512,2]{0,1:T(2,128)}, s32[512,2]{0,1:T(2,128)S(1)}, u32[]{:S(2)}) copy-start(s32[512,2]{0,1:T(2,128)S(1)} %get-tuple-element.40) | copy-start | bytes 12292
  9.3 94.4 %copy-start.4 = (f32[384]{0:T(512)}, f32[384]{0:T(512)S(1)}, u32[]{:S(2)}) copy-start(f32[384]{0:T(512)S(1)} %dynamic-slice_reduce_fusion.2) | copy-start | bytes 4612
  72.3 31.3 %copy-start.5 = (f32[512]{0:T(512)}, f32[512]{0:T(512)S(1)}, u32[]{:S(2)}) copy-start(f32[512]{0:T(512)S(1)} %add_rsqrt_fusion.1) | copy-start | bytes 6148
  77.2 26.5 %copy-start.10 = (pred[2,512]{1,0:T(4,128)(4,1)}, pred[2,512]{1,0:T(4,128)(4,1)S(1)}, u32[]{:S(2)}) copy-start(pred[2,512]{1,0:T(4,128)(4,1)S(1)} %get-tuple-element.44) | copy-start | bytes 3076
  78.3 0.6 copy-start.8
  98.5 4.3 collective-permute-start
  103.6 165.5 %reduce-scatter.7.cloned.1.call-start = ((), (), s32[]{:S(2)}) async-start(), calls=%async_computation.8 | async-start | bytes 3342336
  188.1 106.7 %copy-start.1 = (bf16[512,384]{1,0:T(8,128)(2,1)S(1)}, bf16[512,384]{1,0:T(8,128)(2,1)}, u32[]{:S(2)}) copy-start(bf16[512,384]{1,0:T(8,128)(2,1)} %param.14) | copy-start | bytes 1179652
  188.1 266.8 %all-gather.5.cloned.1.call-start = ((), (), s32[]{:S(2)}) async-start(), calls=%async_computation.7 | async-start | bytes 3342336 | tf_op jit(solution)/shard_map/all_gather | solution.py:74
  190.8 0.6 copy-start.6
  192.0 107.1 %copy-start.7 = (pred[512]{0:T(512)(128)(4,1)S(1)}, pred[512]{0:T(512)(128)(4,1)}, u32[]{:S(2)}) copy-start(pred[512]{0:T(512)(128)(4,1)} %copy-done.6) | copy-start | bytes 1540
  273.1 3.9 collective-permute-start.1
  296.0 18.2 %collective-permute-start.2 = (bf16[512,384]{1,0:T(8,128)(2,1)S(1)}, bf16[512,384]{1,0:T(8,128)(2,1)S(1)}, u32[]{:S(2)}, u32[]{:S(2)}) collective-permute-start(bf16[512,384]{1,0:T(8,128)(2,1)S(1)} %fusion.19), channel_id=1, source_target_pairs={{0,64},{32,96},{64,128},{96,160},{128,192},{160,224},{192,0},{224,... | collective-permute-start | bytes 1179656 | tf_op jit(solution)/shard_map/ppermute | solution.py:21
  394.6 7.2 %collective-permute-start.3 = (bf16[1,128,384]{2,1,0:T(8,128)(2,1)S(1)}, bf16[1,128,384]{2,1,0:T(8,128)(2,1)S(1)}, u32[]{:S(2)}, u32[]{:S(2)}) collective-permute-start(bf16[1,128,384]{2,1,0:T(8,128)(2,1)S(1)} %bitcast.192), channel_id=1, source_target_pairs={{0,32},{32,0},{64,96},{96,64},{128,160},{160,128},{192,224},{224,1... | collective-permute-start | bytes 294920 | tf_op jit(solution)/shard_map/ppermute | solution.py:16
  402.5 164.9 %reduce-scatter.9.cloned.1.call-start = ((), (), s32[]{:S(2)}) async-start(), calls=%async_computation.9 | async-start | bytes 3342336
  486.4 2.1 copy-start.3
  486.4 106.1 %copy-start.9 = (s32[2,512]{1,0:T(2,128)S(1)}, s32[2,512]{1,0:T(2,128)}, u32[]{:S(2)}) copy-start(s32[2,512]{1,0:T(2,128)} %fusion.83) | copy-start | bytes 12292
  571.3 3.8 collective-permute-start.4
Sparse Core Ops, SparseCore 0:
  103.7 53.5 all-gather.2
  188.2 80.8 reduce-scatter.6
  402.6 52.2 all-gather.4
  486.5 80.8 reduce-scatter.8
where the time goes:
time: 603 us; the launch traced here: 601 us
  waiting for transfers between devices  280 us (46%)
  blocking collectives  173 us (29%)
  local copies, waits for them, and re-layouts  65.9 us (11%)
  matrix products  33.2 us (6%)
  other arithmetic  24.3 us (4%)
  between operations  13.3 us (2%)
  starting transfers between devices  11 us (2%)
    unnamed x6, waiting for transfers between devices  154 us
    psum x2, blocking collectives, moe_layer(): lax.psum((jnp.sum(as_float * as_float, axis=1), part_logits), 'tensor')  119 us
    all_gather x2, waiting for transfers between devices, moe_layer(): feature_piece = lax.all_gather(held_rows, 'tensor', axis=2, tiled=True)  106 us
    unnamed x39, local copies, waits for them, and re-layouts  56.4 us
    all_to_all x2, blocking collectives, moe_layer(): lax.all_to_all(widened.reshape(expert_count, CAP, feature_count), 'expert...  36.8 us
    all_to_all x2, blocking collectives, moe_layer(): lax.all_to_all(slab_out, 'expert', split_axis=1, concat_axis=0, tiled=True)  17.2 us
    dot_general x2, matrix products, moe_layer(): jnp.einsum('snf,sfd->snd', hidden, down_w, preferred_element_type=jnp.flo...  16 us
    ppermute x1, waiting for transfers between devices, from_behind(): return lax.ppermute(x, axis, [(i, (i + by) % peers) for i in range(peers)])  14.5 us
  transfers between devices with their start and end apart: 9, of which 8 were waited for; matrix products, arithmetic and copies ran while one was open for 2% of the time, Pallas kernels for 0%

commit v1 on v0

--- a/solution.py
+++ b/solution.py
@@ -71,7 +71,9 @@
     )
     partner = swapped(arrived, "section", 0)
     held_rows = jnp.concatenate([arrived, partner], axis=1)
-    feature_piece = lax.all_gather(held_rows, "tensor", axis=2, tiled=True)
+    feature_piece = jnp.concatenate(
+        lax.all_to_all(jnp.stack([held_rows] * lax.axis_size("tensor")), "tensor", 0, 0), axis=2
+    )
     col_count = feature_piece.shape[2]
     gate_part = lax.slice_in_dim(gate_w, 0, col_count, axis=1)
     up_part = lax.slice_in_dim(up_w, 0, col_count, axis=1)

time: 603 us -> 579 us (0.960)
  waiting for transfers between devices: 280 us -> 171 us
  blocking collectives: 173 us -> 256 us
  local copies, waits for them, and re-layouts: 65.9 us -> 72.7 us
    all_gather x2 -> x0, waiting for transfers between devices: 106 us -> none  [moe_layer(): feature_piece = lax.all_gather(held_rows, 'tensor', axis=2, tiled=True)]
    all_to_all x0 -> x2, blocking collectives: none -> 82.9 us  [moe_layer(): lax.all_to_all(jnp.stack([held_rows] * lax.axis_size('tensor')), 'tensor'...]
    unnamed x39 -> x47, local copies, waits for them, and re-layouts: 56.4 us -> 59.8 us
    unnamed x6 -> x4, waiting for transfers between devices: 154 us -> 151 us
  transfers between devices with their start and end apart: 9 -> 7, of which waited for: 8 -> 6; matrix products, arithmetic and copies ran while one was open for 2% -> 2% of each run, Pallas kernels for 0% -> 0%
where the time goes in v1:
time: 579 us; the launch traced here: 576 us
  blocking collectives  256 us (44%)
  waiting for transfers between devices  171 us (30%)
  local copies, waits for them, and re-layouts  72.7 us (13%)
  matrix products  27.6 us (5%)
  other arithmetic  23.7 us (4%)
  between operations  13.6 us (2%)
  starting transfers between devices  11 us (2%)
    unnamed x4, waiting for transfers between devices  151 us
    psum x2, blocking collectives, moe_layer(): lax.psum((jnp.sum(as_float * as_float, axis=1), part_logits), 'tensor')  119 us
    all_to_all x2, blocking collectives, moe_layer(): lax.all_to_all(jnp.stack([held_rows] * lax.axis_size('tensor')), 'tensor'...  82.9 us
    unnamed x47, local copies, waits for them, and re-layouts  59.8 us
    all_to_all x2, blocking collectives, moe_layer(): lax.all_to_all(widened.reshape(expert_count, CAP, feature_count), 'expert...  36.8 us
    all_to_all x2, blocking collectives, moe_layer(): lax.all_to_all(slab_out, 'expert', split_axis=1, concat_axis=0, tiled=True)  17.2 us
    dot_general x2, matrix products, moe_layer(): jnp.einsum('snf,sfd->snd', hidden, down_w, preferred_element_type=jnp.flo...  16.1 us
    ppermute x1, waiting for transfers between devices, from_behind(): return lax.ppermute(x, axis, [(i, (i + by) % peers) for i in range(peers)])  14.5 us
  transfers between devices with their start and end apart: 7, of which 6 were waited for; matrix products, arithmetic and copies ran while one was open for 2% of the time, Pallas kernels for 0%

profile of v1, /device:TPU:1, one launch (start us, length us, event | category | flops | bytes accessed | tf_op | source)
XLA Modules:
  0.0 576.2 jit_solution(17658424512175005526)
XLA Ops:
  6.5 1.3 fusion.34
  9.3 1.8 fusion.29
  11.1 61.2 %all-reduce.1 = (f32[512]{0:T(512)S(1)}, f32[512,8]{0,1:T(8,128)}) all-reduce(f32[512]{0:T(512)S(1)} %fusion.34, f32[512,8]{0,1:T(8,128)S(1)} %fusion.29), channel_id=1, replica_groups=mesh['section'=8,'expert'=2,'tensor'=16] {'tensor'}, use_global_device_ids=true, to_apply=%region_4.6 | all-reduce | flops 4608 | bytes 36864 | tf_op jit(solution)/shard_map/psum | solution.py:53
  72.3 1.0 dynamic-slice_reduce_fusion
  74.6 2.6 select_compare_fusion.1
  78.9 1.3 convolution_convert_fusion.3
  80.3 18.3 %all_to_all.52 = bf16[2,64,384]{2,1,0:T(8,128)(2,1)S(1)} all-to-all(bf16[2,64,384]{2,1,0:T(8,128)(2,1)S(1)} %convolution_convert_fusion.3), channel_id=1, replica_groups=mesh['section'=8,'expert'=2,'tensor'=16] {'expert'}, dimensions={0} | all-to-all | bytes 196608 | tf_op jit(solution)/shard_map/all_to_all | solution.py:65
  98.6 1.6 collective-permute-start
  100.2 2.7 collective-permute-done
  103.4 41.5 %all_to_all.53 = bf16[16,1,256,384]{2,3,1,0:T(8,128)(2,1)S(1)} all-to-all(bf16[16,1,256,384]{2,3,1,0:T(8,128)(2,1)S(1)} %stack.4), channel_id=1, replica_groups=mesh['section'=8,'expert'=2,'tensor'=16] {'tensor'}, dimensions={0} | all-to-all | bytes 6291456 | tf_op jit(solution)/shard_map/all_to_all | solution.py:75
  144.9 1.7 copy-done.1
  146.6 1.0 fusion.10
  147.6 8.0 %fusion = bf16[1,256,6144]{2,1,0:T(8,128)(2,1)} fusion(bf16[1,1,256,6144]{3,2,1,0:T(8,128)(2,1)S(1)} %copy-done, bf16[256,6144]{0,1:T(8,128)(2,1)} %bitcast.191, bf16[1,1,6144,256]{3,2,1,0:T(8,128)(2,1)} %param.18, f32[256,256]{1,0:T(8,128)S(1)} %fusion.10), kind=kOutput, calls=%fused_computation.2 | convolution fusion | flops 1612578816 | bytes 12845056 | tf_op jit(solution)/shard_map/snf,sfd->snd/dot_general | solution.py:85
  155.7 13.9 %copy.23 = bf16[1,256,6144]{1,0,2:T(2,128)(2,1)} copy(bf16[1,256,6144]{2,1,0:T(8,128)(2,1)} %fusion) | data formatting | bytes 6291456
  169.6 5.0 copy.44
  174.7 2.5 select_compare_fusion
  179.2 0.7 slice_bitcast_fusion.3
  180.5 74.4 %reduce-scatter.7.cloned.1.call-done = bf16[384,256]{1,0:T(8,128)(2,1)} async-done(((bf16[6144,256]{1,0:T(8,128)(2,1)}), bf16[384,256]{1,0:T(8,128)(2,1)}) %reduce-scatter.7.cloned.1.call-update) | async-done | bytes 196624
  254.9 1.1 reshape_bitcast_fusion.1
  256.1 1.1 fusion.109
  257.2 1.7 copy.32
  258.9 1.3 collective-permute-start.1
  260.3 0.8 reduce-window.27
  261.1 1.7 copy.31
  262.8 1.0 add_convert_fusion.1
  263.8 0.8 copy.46
  265.2 2.8 reduce.13
  268.0 1.6 reshape.237
  269.5 8.5 %all_to_all.54 = bf16[2,2,12288]{2,1,0:T(2,128)(2,1)} all-to-all(bf16[2,2,12288]{2,1,0:T(2,128)(2,1)} %reshape.237), channel_id=1, replica_groups=mesh['section'=8,'expert'=2,'tensor'=16] {'expert'}, dimensions={0} | all-to-all | bytes 196608 | tf_op jit(solution)/shard_map/all_to_all | solution.py:96
  278.1 1.7 reshape.238
  279.7 0.9 copy.28
  280.7 1.2 fusion.15
  281.9 2.5 collective-permute-start.2
  285.7 14.5 %collective-permute-done.2 = bf16[512,384]{1,0:T(8,128)(2,1)S(1)} collective-permute-done((bf16[512,384]{1,0:T(8,128)(2,1)S(1)}, bf16[512,384]{1,0:T(8,128)(2,1)S(1)}, u32[]{:S(2)}, u32[]{:S(2)}) %collective-permute-start.2) | collective-permute-done | bytes 393248 | tf_op jit(solution)/shard_map/ppermute | solution.py:21
  301.0 1.5 fusion.31
  302.5 58.1 %all-reduce = (f32[512]{0:T(512)}, f32[512,8]{0,1:T(8,128)}) all-reduce(f32[512]{0:T(512)} %fusion.35, f32[512,8]{0,1:T(8,128)S(1)} %fusion.31), channel_id=1, replica_groups=mesh['section'=8,'expert'=2,'tensor'=16] {'tensor'}, use_global_device_ids=true, to_apply=%region_12.14 | all-reduce | flops 4608 | bytes 36864 | tf_op jit(solution)/shard_map/psum | solution.py:53
  361.2 1.0 convolution_convert_fusion.2
  362.2 18.4 %all_to_all.55 = bf16[2,64,384]{2,1,0:T(8,128)(2,1)S(1)} all-to-all(bf16[2,64,384]{2,1,0:T(8,128)(2,1)S(1)} %convolution_convert_fusion.2), channel_id=1, replica_groups=mesh['section'=8,'expert'=2,'tensor'=16] {'expert'}, dimensions={0} | all-to-all | bytes 196608 | tf_op jit(solution)/shard_map/all_to_all | solution.py:65
  380.7 4.3 collective-permute-start.3
  384.9 2.8 collective-permute-done.3
  388.5 1.7 copy.20
  390.2 1.2 stack.5
  391.4 41.5 %all_to_all.56 = bf16[16,1,256,384]{2,3,1,0:T(8,128)(2,1)S(1)} all-to-all(bf16[16,1,256,384]{2,3,1,0:T(8,128)(2,1)S(1)} %stack.5), channel_id=1, replica_groups=mesh['section'=8,'expert'=2,'tensor'=16] {'tensor'}, dimensions={0} | all-to-all | bytes 6291456 | tf_op jit(solution)/shard_map/all_to_all | solution.py:75
  432.9 1.7 copy-done.2
  434.6 1.7 fusion.8
  436.3 8.0 %fusion.1 = bf16[1,256,6144]{2,1,0:T(8,128)(2,1)} fusion(bf16[1,1,256,6144]{3,2,1,0:T(8,128)(2,1)S(1)} %copy-done, bf16[256,6144]{0,1:T(8,128)(2,1)} %bitcast.193, bf16[1,1,6144,256]{3,2,1,0:T(8,128)(2,1)} %param.18, f32[256,256]{1,0:T(8,128)} %fusion.8), kind=kOutput, calls=%fused_computation.3 | convolution fusion | flops 1612578816 | bytes 12845056 | tf_op jit(solution)/shard_map/snf,sfd->snd/dot_general | solution.py:85
  444.3 13.9 %copy.25 = bf16[1,256,6144]{1,0,2:T(2,128)(2,1)} copy(bf16[1,256,6144]{2,1,0:T(8,128)(2,1)} %fusion.1) | data formatting | bytes 6291456
  458.3 5.0 copy.43
  463.3 1.3 slice_bitcast_fusion.1
  465.4 76.9 %reduce-scatter.9.cloned.1.call-done = bf16[384,256]{1,0:T(8,128)(2,1)} async-done(((bf16[6144,256]{1,0:T(8,128)(2,1)}), bf16[384,256]{1,0:T(8,128)(2,1)}) %reduce-scatter.9.cloned.1.call-update) | async-done | bytes 196624
  542.3 1.1 reshape_bitcast_fusion
  543.4 1.1 fusion.108
  544.6 1.7 copy.34
  546.2 1.3 collective-permute-start.4
  547.5 0.7 fusion.91
  548.2 1.7 copy.33
  550.0 1.0 add_convert_fusion
  551.0 0.8 copy.45
  551.8 2.8 reduce.14
  554.6 1.6 reshape.239
  556.2 8.6 %all_to_all.57 = bf16[2,2,12288]{2,1,0:T(2,128)(2,1)} all-to-all(bf16[2,2,12288]{2,1,0:T(2,128)(2,1)} %reshape.239), channel_id=1, replica_groups=mesh['section'=8,'expert'=2,'tensor'=16] {'expert'}, dimensions={0} | all-to-all | bytes 196608 | tf_op jit(solution)/shard_map/all_to_all | solution.py:96
  564.8 1.7 reshape.240
  566.5 0.9 copy.30
  567.4 2.0 fusion.14
  (66 shorter events, 12.8 us)
Async XLA Ops:
  6.5 141.1 %copy-start = (bf16[1,1,256,6144]{3,2,1,0:T(8,128)(2,1)S(1)}, bf16[1,1,256,6144]{3,2,1,0:T(8,128)(2,1)}, u32[]{:S(2)}) copy-start(bf16[1,1,256,6144]{3,2,1,0:T(8,128)(2,1)} %param.19) | copy-start | bytes 9437188
  6.5 248.4 %reduce-scatter.7.cloned.1.call-start = ((), (), s32[]{:S(2)}) async-start(), calls=%async_computation.8 | async-start | bytes 3342336
  8.5 94.4 %copy-start.4 = (s32[512,2]{0,1:T(2,128)}, s32[512,2]{0,1:T(2,128)S(1)}, u32[]{:S(2)}) copy-start(s32[512,2]{0,1:T(2,128)S(1)} %get-tuple-element.40) | copy-start | bytes 12292
  9.3 93.7 %copy-start.6 = (f32[384]{0:T(512)}, f32[384]{0:T(512)S(1)}, u32[]{:S(2)}) copy-start(f32[384]{0:T(512)S(1)} %dynamic-slice_reduce_fusion.2) | copy-start | bytes 4612
  72.3 30.6 %copy-start.7 = (f32[512]{0:T(512)}, f32[512]{0:T(512)S(1)}, u32[]{:S(2)}) copy-start(f32[512]{0:T(512)S(1)} %add_rsqrt_fusion.1) | copy-start | bytes 6148
  77.2 25.7 %copy-start.12 = (pred[2,512]{1,0:T(4,128)(4,1)}, pred[2,512]{1,0:T(4,128)(4,1)S(1)}, u32[]{:S(2)}) copy-start(pred[2,512]{1,0:T(4,128)(4,1)S(1)} %get-tuple-element.44) | copy-start | bytes 3076
  78.3 0.6 copy-start.10
  98.6 4.4 collective-permute-start
  103.4 43.2 %copy-start.13 = (bf16[1,1,6144,256]{3,2,1,0:T(8,128)(2,1)S(1)}, bf16[1,1,6144,256]{3,2,1,0:T(8,128)(2,1)}, u32[]{:S(2)}) copy-start(bf16[1,1,6144,256]{3,2,1,0:T(8,128)(2,1)} %param.17) | copy-start | bytes 9437188
  144.9 1.7 copy-start.1
  174.6 106.0 %copy-start.3 = (bf16[512,384]{1,0:T(8,128)(2,1)S(1)}, bf16[512,384]{1,0:T(8,128)(2,1)}, u32[]{:S(2)}) copy-start(bf16[512,384]{1,0:T(8,128)(2,1)} %param.14) | copy-start | bytes 1179652
  174.6 367.6 %reduce-scatter.9.cloned.1.call-start = ((), (), s32[]{:S(2)}) async-start(), calls=%async_computation.9 | async-start | bytes 3342336
  177.2 0.6 copy-start.8
  178.4 106.7 %copy-start.9 = (pred[512]{0:T(512)(128)(4,1)S(1)}, pred[512]{0:T(512)(128)(4,1)}, u32[]{:S(2)}) copy-start(pred[512]{0:T(512)(128)(4,1)} %copy-done.8) | copy-start | bytes 1540
  258.9 3.9 collective-permute-start.1
  281.9 18.3 %collective-permute-start.2 = (bf16[512,384]{1,0:T(8,128)(2,1)S(1)}, bf16[512,384]{1,0:T(8,128)(2,1)S(1)}, u32[]{:S(2)}, u32[]{:S(2)}) collective-permute-start(bf16[512,384]{1,0:T(8,128)(2,1)S(1)} %fusion.15), channel_id=1, source_target_pairs={{0,64},{32,96},{64,128},{96,160},{128,192},{160,224},{192,0},{224,... | collective-permute-start | bytes 1179656 | tf_op jit(solution)/shard_map/ppermute | solution.py:21
  380.7 7.1 %collective-permute-start.3 = (bf16[1,128,384]{2,1,0:T(8,128)(2,1)S(1)}, bf16[1,128,384]{2,1,0:T(8,128)(2,1)S(1)}, u32[]{:S(2)}, u32[]{:S(2)}) collective-permute-start(bf16[1,128,384]{2,1,0:T(8,128)(2,1)S(1)} %bitcast.200), channel_id=1, source_target_pairs={{0,32},{32,0},{64,96},{96,64},{128,160},{160,128},{192,224},{224,1... | collective-permute-start | bytes 294920 | tf_op jit(solution)/shard_map/ppermute | solution.py:16
  391.4 43.1 %copy-start.14 = (bf16[1,1,6144,256]{3,2,1,0:T(8,128)(2,1)S(1)}, bf16[1,1,6144,256]{3,2,1,0:T(8,128)(2,1)}, u32[]{:S(2)}) copy-start(bf16[1,1,6144,256]{3,2,1,0:T(8,128)(2,1)} %param.17) | copy-start | bytes 9437188
  432.9 1.7 copy-start.2
  463.3 2.1 copy-start.5
  463.3 104.1 %copy-start.11 = (s32[2,512]{1,0:T(2,128)S(1)}, s32[2,512]{1,0:T(2,128)}, u32[]{:S(2)}) copy-start(s32[2,512]{1,0:T(2,128)} %fusion.89) | copy-start | bytes 12292
  546.2 3.8 collective-permute-start.4
Sparse Core Ops, SparseCore 0:
  174.8 80.1 reduce-scatter.6
  463.4 78.8 reduce-scatter.8
